TPU v7x, 256 devices: a whole 4x4x8 slice. The times are simulated.
256 devices in a mesh: pair: 4 (over y_lo, core), col: 64 (over y_hi, x, z).
Axes of the slice: x: 4, y: 4 (y_hi: 2, y_lo: 2; y = y_hi * 2 + y_lo), z: 8, core: 2. Of those that a mesh axis runs over, the one named last changes fastest.
Arguments:
- amplitudes: bfloat16 [1536, 4096], P('pair', 'col'), may hold values from -6 to 6
- integrals: bfloat16 [4096, 81920], P('pair', 'col'), may hold values from -0.25 to 0.25
- irrep_start: int32 [9], replicated, may hold values from 0 to 4096, as said below
- pair_irrep: int32 [1536], P('pair'), may hold values from 0 to 7
Outputs:
- ladder: bfloat16 [1536, 81920], P('pair', 'col')
Inputs may be any that keep to these rules, and one draw needn't show every extreme that they name: Strictly rising multiples of 128; the first is 0 and the last is 4096; irrep j owns rows irrep_start[j] to irrep_start[j+1] - 1.
All inputs are finite; a program needn't handle non-finite values.
Results may differ from a plain program's by a relative error of at most 0.001.
Values may be sent and summed in bfloat16 or wider, within the bound.
A program may use at most 64 MiB of HBM per device.

v0:
```python
import jax
import jax.numpy as jnp
from jax import lax
from jax.sharding import PartitionSpec as P


def per_device(amplitudes, integrals, irrep_start, pair_irrep):
    local_rows = amplitudes.shape[1]
    first_row = lax.axis_index("col") * local_rows
    rows = first_row + jnp.arange(local_rows, dtype=jnp.int32)
    row_irrep = jnp.sum((rows[:, None] >= irrep_start[None, 1:8]).astype(jnp.int32), axis=1)
    keep = pair_irrep[:, None] == row_irrep[None, :]
    masked = jnp.where(keep, amplitudes, jnp.zeros_like(amplitudes))
    full_amp = lax.all_gather(masked, "col", axis=1, tiled=True)
    blocks = lax.all_to_all(full_amp, "pair", split_axis=1, concat_axis=0, tiled=True)
    summed = lax.psum_scatter(
        jnp.dot(blocks, integrals, preferred_element_type=jnp.float32),
        "pair",
        scatter_dimension=0,
        tiled=True,
    )
    return summed.astype(jnp.bfloat16)


def solution(mesh):
    placed = (P("pair", "col"), P("pair", "col"), P(), P("pair"))
    return jax.shard_map(
        per_device, mesh=mesh, in_specs=placed, out_specs=P("pair", "col"), check_vma=False
    )
```

profile of v0, /device:TPU:1, one launch (start us, length us, event | category | flops | bytes accessed | tf_op | source)
XLA Modules:
  0.0 277.6 jit_solution(218470783332346924)
XLA Ops:
  6.5 0.0 copy-start
  6.5 0.0 all-gather.2.cloned.1.call-start
  6.5 0.9 slice.3
  7.4 0.1 convert_reduce_fusion
  7.5 1.5 compare_select_fusion
  9.0 0.0 all-gather.2.cloned.1.call-update
  9.0 0.0 reduce-scatter.2.cloned.1.call-start
  9.1 125.1 %all-gather.2.cloned.1.call-done = bf16[384,4096]{0,1:T(8,128)(2,1)} async-done(((bf16[384,64]{0,1:T(8,128)(2,1)}), bf16[384,4096]{0,1:T(8,128)(2,1)}) %all-gather.2.cloned.1.call-update) | async-done | bytes 3145744 | tf_op jit(solution)/shard_map/all_gather | solution.py:14
  134.2 45.4 %all_to_all.19 = bf16[384,4,1024]{0,2,1:T(8,128)(2,1)} all-to-all(bf16[384,4,1024]{0,2,1:T(8,128)(2,1)} %bitcast.6), channel_id=1, replica_groups=mesh['pair'=4,'col'=64] {'pair'}, dimensions={1} | all-to-all | bytes 6291456 | tf_op jit(solution)/shard_map/all_to_all | solution.py:15
  179.5 4.7 %copy.6 = bf16[4,384,1024]{2,1,0:T(8,128)(2,1)} copy(bf16[4,384,1024]{1,2,0:T(8,128)(2,1)} %bitcast.5) | data formatting | bytes 6291456 | tf_op jit(solution)/shard_map/all_to_all | solution.py:15
  184.3 0.0 copy-done
  184.3 9.2 %fusion = f32[1536,1280]{1,0:T(8,128)} fusion(bf16[1536,1024]{1,0:T(8,128)(2,1)} %bitcast.7, bf16[1024,1280]{1,0:T(8,128)(2,1)S(1)} %copy-done), kind=kOutput, calls=%fused_computation.3 | convolution fusion | flops 4026531840 | bytes 13631488 | tf_op jit(solution)/shard_map/dot_general | solution.py:17
  193.5 0.0 reduce-scatter.2.cloned.1.call-update
  193.5 74.6 %reduce-scatter.2.cloned.1.call-done = f32[384,1280]{1,0:T(8,128)} async-done(((f32[1536,1280]{1,0:T(8,128)}), f32[384,1280]{1,0:T(8,128)}) %reduce-scatter.2.cloned.1.call-update) | async-done | bytes 1966096 | tf_op jit(solution)/shard_map/reduce_scatter | solution.py:16
  268.1 2.6 convert_element_type.7
  (1 shorter events, 0.0 us)
Async XLA Ops:
  6.5 177.7 %copy-start = (bf16[1024,1280]{1,0:T(8,128)(2,1)S(1)}, bf16[1024,1280]{1,0:T(8,128)(2,1)}, u32[]{:S(2)}) copy-start(bf16[1024,1280]{1,0:T(8,128)(2,1)} %param.5) | copy-start | bytes 7864324
  6.5 127.6 %all-gather.2.cloned.1.call-start = ((), (), s32[]{:S(2)}) async-start(), calls=%async_computation.2 | async-start | bytes 3194880 | tf_op jit(solution)/shard_map/all_gather | solution.py:14
  9.0 259.1 %reduce-scatter.2.cloned.1.call-start = ((), (), s32[]{:S(2)}) async-start(), calls=%async_computation.3 | async-start | bytes 9830400 | tf_op jit(solution)/shard_map/reduce_scatter | solution.py:16
Sparse Core Ops, SparseCore 0:
  11.0 123.0 all-gather.1
  193.6 74.4 reduce-scatter.1
where the time goes:
time: 278 us
  waiting for transfers between devices  200 us (72%)
  blocking collectives  45.4 us (16%)
  between operations  13.4 us (5%)
  matrix products  9.23 us (3%)
  local copies, waits for them, and re-layouts  5.62 us (2%)
  other arithmetic  4.18 us (2%)
    all_gather x1, waiting for transfers between devices, per_device(): full_amp = lax.all_gather(masked, 'col', axis=1, tiled=True)  125 us
    reduce_scatter x1, waiting for transfers between devices, per_device(): lax.psum_scatter(jnp.dot(blocks, integrals, preferred_element_type=jnp.fl...  74.6 us
    all_to_all x1, blocking collectives, per_device(): lax.all_to_all(full_amp, 'pair', split_axis=1, concat_axis=0, tiled=True)  45.4 us
    dot_general x1, matrix products, per_device(): jnp.dot(blocks, integrals, preferred_element_type=jnp.float32)  9.23 us
  transfers between devices with their start and end apart: 2, of which 2 were waited for; matrix products, arithmetic and copies ran while one was open for 0% of the time, Pallas kernels for 0%

commit v1 on v0

--- a/solution.py
+++ b/solution.py
@@ -11,7 +11,9 @@
     row_irrep = jnp.sum((rows[:, None] >= irrep_start[None, 1:8]).astype(jnp.int32), axis=1)
     keep = pair_irrep[:, None] == row_irrep[None, :]
     masked = jnp.where(keep, amplitudes, jnp.zeros_like(amplitudes))
-    full_amp = lax.all_gather(masked, "col", axis=1, tiled=True)
+    full_amp = jnp.concatenate(
+        lax.all_to_all(jnp.stack([masked] * lax.axis_size("col")), "col", 0, 0), axis=1
+    )
     blocks = lax.all_to_all(full_amp, "pair", split_axis=1, concat_axis=0, tiled=True)
     summed = lax.psum_scatter(
         jnp.dot(blocks, integrals, preferred_element_type=jnp.float32),

time: 278 us -> 236 us (0.85)
  waiting for transfers between devices: 200 us -> 74 us
  blocking collectives: 45.4 us -> 130 us
    all_gather x1 -> x0, waiting for transfers between devices: 125 us -> none  [per_device(): full_amp = lax.all_gather(masked, 'col', axis=1, tiled=True)]
    all_to_all x0 -> x1, blocking collectives: none -> 87.9 us  [per_device(): lax.all_to_all(jnp.stack([masked] * lax.axis_size('col')), 'col', 0, 0)]
    all_to_all x1, blocking collectives: 45.4 us -> 41.7 us  [per_device(): lax.all_to_all(full_amp, 'pair', split_axis=1, concat_axis=0, tiled=True)]
  transfers between devices with their start and end apart: 2 -> 1, of which waited for: 2 -> 1; matrix products, arithmetic and copies ran while one was open for 0% -> 0% of each run, Pallas kernels for 0% -> 0%
where the time goes in v1:
time: 236 us
  blocking collectives  130 us (55%)
  waiting for transfers between devices  74 us (31%)
  between operations  13.4 us (6%)
  matrix products  9.23 us (4%)
  local copies, waits for them, and re-layouts  6.1 us (3%)
  other arithmetic  3.56 us (2%)
    all_to_all x1, blocking collectives, per_device(): lax.all_to_all(jnp.stack([masked] * lax.axis_size('col')), 'col', 0, 0)  87.9 us
    reduce_scatter x1, waiting for transfers between devices, per_device(): lax.psum_scatter(jnp.dot(blocks, integrals, preferred_element_type=jnp.fl...  74 us
    all_to_all x1, blocking collectives, per_device(): lax.all_to_all(full_amp, 'pair', split_axis=1, concat_axis=0, tiled=True)  41.7 us
    dot_general x1, matrix products, per_device(): jnp.dot(blocks, integrals, preferred_element_type=jnp.float32)  9.23 us
    all_to_all x1, local copies, waits for them, and re-layouts, per_device(): lax.all_to_all(full_amp, 'pair', split_axis=1, concat_axis=0, tiled=True)  4.73 us
  transfers between devices with their start and end apart: 1, of which 1 were waited for; matrix products, arithmetic and copies ran while one was open for 0% of the time, Pallas kernels for 0%

profile of v1, /device:TPU:1, one launch (start us, length us, event | category | flops | bytes accessed | tf_op | source)
XLA Modules:
  0.0 235.9 jit_solution(12534893899338710685)
XLA Ops:
  6.5 0.0 copy-start
  6.5 0.0 reduce-scatter.2.cloned.1.call-start
  6.5 0.9 slice.3
  7.4 0.1 convert_reduce_fusion
  7.5 0.9 compare_select_fusion
  8.4 0.5 stack.2
  8.9 87.9 %all_to_all.24 = bf16[64,384,64]{1,2,0:T(8,128)(2,1)S(1)} all-to-all(bf16[64,384,64]{1,2,0:T(8,128)(2,1)S(1)} %stack.2), channel_id=1, replica_groups=mesh['pair'=4,'col'=64] {'col'}, dimensions={0} | all-to-all | bytes 6291456 | tf_op jit(solution)/shard_map/all_to_all | solution.py:15
  96.8 41.7 %all_to_all.25 = bf16[384,4,1024]{0,2,1:T(8,128)(2,1)} all-to-all(bf16[384,4,1024]{0,2,1:T(8,128)(2,1)S(1)} %bitcast.7), channel_id=1, replica_groups=mesh['pair'=4,'col'=64] {'pair'}, dimensions={1} | all-to-all | bytes 6291456 | tf_op jit(solution)/shard_map/all_to_all | solution.py:17
  138.5 4.7 %copy.7 = bf16[4,384,1024]{2,1,0:T(8,128)(2,1)} copy(bf16[4,384,1024]{1,2,0:T(8,128)(2,1)} %bitcast.8) | data formatting | bytes 6291456 | tf_op jit(solution)/shard_map/all_to_all | solution.py:17
  143.2 0.0 copy-done
  143.2 9.2 %fusion = f32[1536,1280]{1,0:T(8,128)} fusion(bf16[1536,1024]{1,0:T(8,128)(2,1)} %bitcast.9, bf16[1024,1280]{1,0:T(8,128)(2,1)S(1)} %copy-done), kind=kOutput, calls=%fused_computation.3 | convolution fusion | flops 4026531840 | bytes 13631488 | tf_op jit(solution)/shard_map/dot_general | solution.py:19
  152.4 0.0 reduce-scatter.2.cloned.1.call-update
  152.5 74.0 %reduce-scatter.2.cloned.1.call-done = f32[384,1280]{1,0:T(8,128)} async-done(((f32[1536,1280]{1,0:T(8,128)}), f32[384,1280]{1,0:T(8,128)}) %reduce-scatter.2.cloned.1.call-update) | async-done | bytes 1966096 | tf_op jit(solution)/shard_map/reduce_scatter | solution.py:18
  226.4 2.6 %convert_element_type.7 = bf16[384,1280]{1,0:T(8,128)(2,1)} convert(f32[384,1280]{1,0:T(8,128)} %reduce-scatter.2.cloned.1.call-done) | non-fusion elementwise | flops 491520 | bytes 2949120 | tf_op jit(solution)/shard_map/convert_element_type | solution.py:24
  (1 shorter events, 0.0 us)
Async XLA Ops:
  6.5 136.7 %copy-start = (bf16[1024,1280]{1,0:T(8,128)(2,1)S(1)}, bf16[1024,1280]{1,0:T(8,128)(2,1)}, u32[]{:S(2)}) copy-start(bf16[1024,1280]{1,0:T(8,128)(2,1)} %param.5) | copy-start | bytes 7864324
  6.5 219.9 %reduce-scatter.2.cloned.1.call-start = ((), (), s32[]{:S(2)}) async-start(), calls=%async_computation.3 | async-start | bytes 9830400 | tf_op jit(solution)/shard_map/reduce_scatter | solution.py:18
Sparse Core Ops, SparseCore 0:
  152.6 73.8 reduce-scatter.1
